TPU v7x, 256 devices: a whole 4x4x8 slice. The times are simulated.
256 devices in a mesh: group: 32 (over y, z), inner: 8 (over x, core).
Axes of the slice: x: 4, y: 4, z: 8, core: 2. Of those that a mesh axis runs over, the one named last changes fastest.
Arguments:
- tokens: bfloat16 [4096, 7168], P('group', 'inner'), may hold values from -6 to 6
- routes: int32 [4096, 4], P('group'), may hold values from 0 to 31, all different within a row; in each aligned block of 128 rows (0 to 127, 128 to 255, ...) at most 24 rows name the same one
- gate_weights: float32 [4096, 4], P('group'), may hold values from 0.1 to 1
- w_gate: bfloat16 [32, 7168, 2048], P('group', None, 'inner'), may hold values from -0.0625 to 0.0625
- w_up: bfloat16 [32, 7168, 2048], P('group', None, 'inner'), may hold values from -0.0625 to 0.0625
- w_down: bfloat16 [32, 2048, 7168], P('group', 'inner'), may hold values from -0.125 to 0.125
Outputs:
- moe_out: bfloat16 [4096, 7168], P('group', 'inner')
Inputs may be any that keep to these rules, and one draw needn't show every extreme that they name: `routes`: each row names 4 different expert groups. Within each aligned block of 128 rows (the rows of one index of group) no group is named by more than 24 rows, and in some blocks one group is named by exactly 24 rows.
All inputs are finite; a program needn't handle non-finite values.
Results may differ from a plain program's by a relative error of at most 0.014.
Values may be sent and summed in bfloat16 or wider, within the bound.
A program may use at most 128 MiB of HBM per device.

v0:
```python
import jax
import jax.numpy as jnp
from jax import lax
from jax.sharding import PartitionSpec as P


def layout(routes, groups, capacity):
    group_ids = jnp.arange(groups, dtype=jnp.int32)
    onehot = routes[:, :, None] == group_ids[None, None, :]
    chosen = jnp.sum(onehot.astype(jnp.int32), axis=1)
    slot_of = jnp.cumsum(chosen, axis=0) - 1
    slot_ids = jnp.arange(capacity, dtype=jnp.int32)
    placing = (chosen.T[:, None, :] == 1) & (slot_of.T[:, None, :] == slot_ids[None, :, None])
    pick_slot = jnp.take_along_axis(slot_of, routes, axis=1)
    pick_index = routes * capacity + pick_slot
    return (placing, pick_index)


def pack_rows(placing, token_rows):
    packed = jnp.einsum(
        "hct,td->hcd", placing.astype(jnp.bfloat16), token_rows, preferred_element_type=jnp.float32
    )
    return packed.astype(jnp.bfloat16)


def combine(pick_index, gate_weights, returned):
    flat_rows = returned.reshape(returned.shape[0] * returned.shape[1], returned.shape[2])
    taken = jnp.take(flat_rows, pick_index, axis=0).astype(jnp.float32)
    return jnp.sum(taken * gate_weights[:, :, None], axis=1)


def local(tokens, routes, gate_weights, w_gate, w_up, w_down):
    groups = lax.axis_size("group")
    shard_rows = tokens.shape[0]
    capacity = shard_rows * routes.shape[1] * 3 // (2 * groups)
    placing, pick_index = layout(routes, groups, capacity)
    gate_mat = w_gate[0]
    up_mat = w_up[0]
    down_mat = w_down[0]
    arrived = lax.all_to_all(
        pack_rows(placing, tokens), "group", split_axis=0, concat_axis=0, tiled=True
    )
    feature_part = lax.all_gather(arrived, "inner", axis=2, tiled=True)
    gate_add = jnp.einsum("hck,kf->hcf", feature_part, gate_mat, preferred_element_type=jnp.float32)
    up_add = jnp.einsum("hck,kf->hcf", feature_part, up_mat, preferred_element_type=jnp.float32)
    hidden = (jax.nn.silu(gate_add) * up_add).astype(jnp.bfloat16)
    partial_value = jnp.einsum(
        "hcf,fd->hcd", hidden, down_mat, preferred_element_type=jnp.float32
    ).astype(jnp.bfloat16)
    returned = lax.all_to_all(partial_value, "group", split_axis=0, concat_axis=0, tiled=True)
    combined = combine(pick_index, gate_weights, returned)
    result = lax.psum_scatter(
        combined.astype(jnp.bfloat16), "inner", scatter_dimension=1, tiled=True
    )
    return result


def solution(mesh):
    placed = (
        P("group", "inner"),
        P("group", None),
        P("group", None),
        P("group", None, "inner"),
        P("group", None, "inner"),
        P("group", "inner", None),
    )
    return jax.shard_map(
        local, mesh=mesh, in_specs=placed, out_specs=P("group", "inner"), check_vma=False
    )
```

profile of v0, /device:TPU:1, one launch (start us, length us, event | category | flops | bytes accessed | tf_op | source)
XLA Modules:
  0.0 493.6 jit_solution(10013440760367725060)
XLA Ops:
  6.5 0.7 convert_reduce_fusion
  7.4 0.2 reduce_window_sum.11
  7.6 0.5 convolution_convert_fusion.1
  8.2 45.1 %all_to_all.10 = bf16[32,24,896]{2,1,0:T(8,128)(2,1)} all-to-all(bf16[32,24,896]{2,1,0:T(8,128)(2,1)S(1)} %convolution_convert_fusion.1), channel_id=1, replica_groups=mesh['group'=32,'inner'=8] {'group'}, dimensions={0} | all-to-all | bytes 2752512 | tf_op jit(solution)/shard_map/all_to_all | solution.py:40
  53.3 63.1 %all-gather.2.cloned.1.call-done = bf16[32,24,7168]{2,1,0:T(8,128)(2,1)} async-done(((bf16[32,24,896]{2,1,0:T(8,128)(2,1)}), bf16[32,24,7168]{2,1,0:T(8,128)(2,1)}) %all-gather.2.cloned.1.call-update) | async-done | bytes 11010064 | tf_op jit(solution)/shard_map/all_gather | solution.py:43
  116.3 7.0 %fusion.3 = f32[32,24,256]{2,1,0:T(8,128)S(1)} fusion(bf16[32,24,7168]{2,1,0:T(8,128)(2,1)} %all-gather.2.cloned.1.call-done, bf16[1,7168,256]{2,1,0:T(8,128)(2,1)} %param.9), kind=kOutput, calls=%fused_computation.7 | convolution fusion | flops 2818572288 | bytes 15466496 | tf_op jit(solution)/shard_map/hck,kf->hcf/dot_general | solution.py:44
  123.3 1.3 copy-done.5
  124.7 1.0 copy-done.6
  125.7 3.2 fusion.8
  129.0 5.7 %convolution_convert_fusion = bf16[32,24,7168]{2,1,0:T(8,128)(2,1)} fusion(bf16[32,24,256]{2,1,0:T(8,128)(2,1)S(1)} %fusion.8, bf16[1,256,7168]{2,1,0:T(8,128)(2,1)S(1)} %copy-done.2), kind=kOutput, calls=%fused_computation.3 | convolution fusion | flops 2824077312 | bytes 15073280 | tf_op jit(solution)/shard_map/hcf,fd->hcd/dot_general | solution.py:47
  134.7 9.8 %all-to-all-start.1 = ((bf16[32,24,7168]{2,1,0:T(8,128)(2,1)}), bf16[32,24,7168]{2,1,0:T(8,128)(2,1)}, u32[]{:S(2)}, u32[]{:S(2)}) async-start(bf16[32,24,7168]{2,1,0:T(8,128)(2,1)} %convolution_convert_fusion), calls=%async_computation.1 | async-start | bytes 22020096 | tf_op jit(solution)/shard_map/all_to_all | solution.py:50
  144.5 0.2 reduce-scatter.4.cloned.1.call-start
  144.7 0.1 copy.45
  145.0 3.8 gather_fusion.1
  149.0 0.1 copy.49
  149.2 0.1 copy.47
  149.3 0.1 copy.50
  149.4 240.2 %all-to-all-done.1 = bf16[32,24,7168]{2,1,0:T(8,128)(2,1)} async-done(((bf16[32,24,7168]{2,1,0:T(8,128)(2,1)}), bf16[32,24,7168]{2,1,0:T(8,128)(2,1)}, u32[]{:S(2)}, u32[]{:S(2)}) %all-to-all-start.1) | async-done | bytes 11010080 | tf_op jit(solution)/shard_map/all_to_all | solution.py:50
  389.6 19.3 %gather_fusion = bf16[512,7168]{1,0:T(8,128)(2,1)} fusion(bf16[768,7168]{1,0:T(8,128)(2,1)} %bitcast.10, s32[1024]{0:T(1024)S(1)} %pad_clamp_fusion), kind=kCustom, calls=%fused_computation | custom fusion | bytes 14682112 | tf_op jit(solution)/shard_map/jit(_take)/gather | solution.py:28
  408.9 12.7 %reshape.25 = bf16[128,4,7168]{2,1,0:T(4,128)(2,1)} reshape(bf16[512,7168]{1,0:T(8,128)(2,1)} %gather_fusion) | data formatting | bytes 14680064 | tf_op jit(solution)/shard_map/jit(_take)/gather | solution.py:28
  421.6 12.9 %multiply_reduce_fusion = bf16[128,7168]{1,0:T(8,128)(2,1)S(1)} fusion(f32[128,4]{1,0:T(8,128)S(1)} %copy.50, bf16[128,4,7168]{2,1,0:T(4,128)(2,1)} %reshape.25, pred[128,4]{1,0:T(8,128)(4,1)S(1)} %copy.47), kind=kLoop, calls=%fused_computation.2 | loop fusion | flops 13762560 | bytes 9177600 | tf_op jit(solution)/shard_map/reduce_sum | solution.py:29
  434.5 2.3 copy.51
  436.8 48.2 %reduce-scatter.4.cloned.1.call-done = bf16[896,128]{1,0:T(8,128)(2,1)} async-done(((bf16[7168,128]{1,0:T(8,128)(2,1)}), bf16[896,128]{1,0:T(8,128)(2,1)}) %reduce-scatter.4.cloned.1.call-update) | async-done | bytes 229392
  485.0 1.8 copy.52
  (26 shorter events, 0.6 us)
Async XLA Ops:
  6.5 1.1 copy-start
  6.5 109.8 %all-gather.2.cloned.1.call-start = ((), (), s32[]{:S(2)}) async-start(), calls=%async_computation.3 | async-start | bytes 12386304 | tf_op jit(solution)/shard_map/all_gather | solution.py:43
  116.3 8.4 %copy-start.5 = (bf16[32,24,7168]{2,1,0:T(8,128)(2,1)S(1)}, bf16[32,24,7168]{2,1,0:T(8,128)(2,1)}, u32[]{:S(2)}) copy-start(bf16[32,24,7168]{2,1,0:T(8,128)(2,1)} %all-gather.2.cloned.1.call-done) | copy-start | bytes 33030148
  116.3 9.4 %copy-start.6 = (bf16[1,7168,256]{2,1,0:T(8,128)(2,1)S(1)}, bf16[1,7168,256]{2,1,0:T(8,128)(2,1)}, u32[]{:S(2)}) copy-start(bf16[1,7168,256]{2,1,0:T(8,128)(2,1)} %param.10) | copy-start | bytes 11010052
  125.7 3.2 copy-start.2
  134.7 10.1 %copy-start.3 = (s32[128,4]{0,1:T(4,128)S(1)}, s32[128,4]{0,1:T(4,128)}, u32[]{:S(2)}) copy-start(s32[128,4]{0,1:T(4,128)} %param.7) | copy-start | bytes 6148
  134.7 254.9 %all-to-all-start.1 = ((bf16[32,24,7168]{2,1,0:T(8,128)(2,1)}), bf16[32,24,7168]{2,1,0:T(8,128)(2,1)}, u32[]{:S(2)}, u32[]{:S(2)}) async-start(bf16[32,24,7168]{2,1,0:T(8,128)(2,1)} %convolution_convert_fusion), calls=%async_computation.1 | async-start | bytes 22020096 | tf_op jit(solution)/shard_map/all_to_all | solution.py:50
  144.5 340.5 %reduce-scatter.4.cloned.1.call-start = ((), (), s32[]{:S(2)}) async-start(), calls=%async_computation.4 | async-start | bytes 2064384
  145.0 4.4 copy-start.4
  408.9 77.9 %copy-start.1 = (bf16[128,896]{1,0:T(8,128)(2,1)S(1)}, bf16[128,896]{1,0:T(8,128)(2,1)}, u32[]{:S(2)}) copy-start(bf16[128,896]{1,0:T(8,128)(2,1)} %param.6) | copy-start | bytes 688132
Sparse Core Ops, SparseCore 0:
  53.4 62.8 all-gather.1
  436.9 48.0 reduce-scatter.3
where the time goes:
time: 496 us; the launch traced here: 494 us
  waiting for transfers between devices  351 us (71%)
  blocking collectives  45.1 us (9%)
  local copies, waits for them, and re-layouts  43.2 us (9%)
  matrix products  16.5 us (3%)
  other arithmetic  13.9 us (3%)
  between operations  13.5 us (3%)
  starting transfers between devices  10 us (2%)
    all_to_all x1, waiting for transfers between devices, local(): lax.all_to_all(partial_value, 'group', split_axis=0, concat_axis=0, tiled...  240 us
    all_gather x1, waiting for transfers between devices, local(): feature_part = lax.all_gather(arrived, 'inner', axis=2, tiled=True)  63.1 us
    unnamed x3, waiting for transfers between devices  48.2 us
    all_to_all x1, blocking collectives, local(): lax.all_to_all(pack_rows(placing, tokens), 'group', split_axis=0, concat_...  45.1 us
    gather x2, local copies, waits for them, and re-layouts, combine(): taken = jnp.take(flat_rows, pick_index, axis=0).astype(jnp.float32)  32 us
    reduce_sum x1, other arithmetic, combine(): return jnp.sum(taken * gate_weights[:, :, None], axis=1)  12.9 us
  transfers between devices with their start and end apart: 3, of which 3 were waited for; matrix products, arithmetic and copies ran while one was open for 1% of the time, Pallas kernels for 0%

commit v1 on v0

--- a/solution.py
+++ b/solution.py
@@ -47,12 +47,9 @@
     partial_value = jnp.einsum(
         "hcf,fd->hcd", hidden, down_mat, preferred_element_type=jnp.float32
     ).astype(jnp.bfloat16)
-    returned = lax.all_to_all(partial_value, "group", split_axis=0, concat_axis=0, tiled=True)
-    combined = combine(pick_index, gate_weights, returned)
-    result = lax.psum_scatter(
-        combined.astype(jnp.bfloat16), "inner", scatter_dimension=1, tiled=True
-    )
-    return result
+    summed = lax.psum_scatter(partial_value, "inner", scatter_dimension=2, tiled=True)
+    returned = lax.all_to_all(summed, "group", split_axis=0, concat_axis=0, tiled=True)
+    return combine(pick_index, gate_weights, returned).astype(jnp.bfloat16)
 
 
 def solution(mesh):

time: 496 us -> 417 us (0.84)
  waiting for transfers between devices: 351 us -> 158 us
  local copies, waits for them, and re-layouts: 43.2 us -> 165 us
  other arithmetic: 13.9 us -> 3.1 us
    all_to_all x1, waiting for transfers between devices: 240 us -> 27.9 us  [local(): lax.all_to_all(summed, 'group', split_axis=0, concat_axis=0, tiled=True)]
    unnamed x17 -> x19, local copies, waits for them, and re-layouts: 6.59 us -> 158 us
    gather x2, local copies, waits for them, and re-layouts: 32 us -> 2.26 us  [combine(): taken = jnp.take(flat_rows, pick_index, axis=0).astype(jnp.float32)]
    unnamed x3, waiting for transfers between devices: 48.2 us -> 67.1 us
    reduce_sum x1, other arithmetic: 12.9 us -> 2.13 us  [combine(): return jnp.sum(taken * gate_weights[:, :, None], axis=1)]
where the time goes in v1:
time: 417 us; the launch traced here: 411 us
  local copies, waits for them, and re-layouts  165 us (40%)
  waiting for transfers between devices  158 us (38%)
  blocking collectives  45.1 us (11%)
  matrix products  16.6 us (4%)
  between operations  13.5 us (3%)
  starting transfers between devices  9.79 us (2%)
    unnamed x19, local copies, waits for them, and re-layouts  158 us
    unnamed x3, waiting for transfers between devices  67.1 us
    all_gather x1, waiting for transfers between devices, local(): feature_part = lax.all_gather(arrived, 'inner', axis=2, tiled=True)  63 us
    all_to_all x1, blocking collectives, local(): lax.all_to_all(pack_rows(placing, tokens), 'group', split_axis=0, concat_...  45.1 us
    all_to_all x1, waiting for transfers between devices, local(): lax.all_to_all(summed, 'group', split_axis=0, concat_axis=0, tiled=True)  27.9 us
    all_to_all x1, starting transfers between devices, local(): lax.all_to_all(summed, 'group', split_axis=0, concat_axis=0, tiled=True)  9.75 us
  transfers between devices with their start and end apart: 3, of which 3 were waited for; matrix products, arithmetic and copies ran while one was open for 1% of the time, Pallas kernels for 0%

profile of v1, /device:TPU:1, one launch (start us, length us, event | category | flops | bytes accessed | tf_op | source)
XLA Modules:
  0.0 411.1 jit_solution(16734024208027349280)
XLA Ops:
  6.5 0.7 convert_reduce_fusion
  7.4 0.2 reduce_window_sum.11
  7.6 0.5 convolution_convert_fusion.1
  8.2 45.1 %all_to_all.10 = bf16[32,24,896]{2,1,0:T(8,128)(2,1)} all-to-all(bf16[32,24,896]{2,1,0:T(8,128)(2,1)S(1)} %convolution_convert_fusion.1), channel_id=1, replica_groups=mesh['group'=32,'inner'=8] {'group'}, dimensions={0} | all-to-all | bytes 2752512 | tf_op jit(solution)/shard_map/all_to_all | solution.py:40
  53.3 63.0 %all-gather.2.cloned.1.call-done = bf16[32,24,7168]{2,1,0:T(8,128)(2,1)} async-done(((bf16[32,24,896]{2,1,0:T(8,128)(2,1)}), bf16[32,24,7168]{2,1,0:T(8,128)(2,1)}) %all-gather.2.cloned.1.call-update) | async-done | bytes 11010064 | tf_op jit(solution)/shard_map/all_gather | solution.py:43
  116.3 7.0 %fusion.3 = f32[32,24,256]{2,1,0:T(8,128)S(1)} fusion(bf16[32,24,7168]{2,1,0:T(8,128)(2,1)} %all-gather.2.cloned.1.call-done, bf16[1,7168,256]{2,1,0:T(8,128)(2,1)} %param.9), kind=kOutput, calls=%fused_computation.6 | convolution fusion | flops 2818572288 | bytes 15466496 | tf_op jit(solution)/shard_map/hck,kf->hcf/dot_general | solution.py:44
  123.3 1.3 copy-done.5
  124.7 1.0 copy-done.6
  125.7 3.2 fusion.8
  129.0 5.8 %convolution_convert_fusion = bf16[32,24,7168]{2,1,0:T(8,128)(2,1)} fusion(bf16[32,24,256]{2,1,0:T(8,128)(2,1)S(1)} %fusion.8, bf16[1,256,7168]{2,1,0:T(8,128)(2,1)S(1)} %copy-done.2), kind=kOutput, calls=%fused_computation.2 | convolution fusion | flops 2824077312 | bytes 15073280 | tf_op jit(solution)/shard_map/hcf,fd->hcd/dot_general | solution.py:47
  134.8 51.3 %copy.51 = bf16[32,24,7168]{1,0,2:T(8,128)(2,1)} copy(bf16[32,24,7168]{2,1,0:T(8,128)(2,1)} %convolution_convert_fusion) | data formatting | bytes 22020096
  186.1 81.1 %reshape.49 = bf16[7168,768]{1,0:T(8,128)(2,1)} reshape(bf16[7168,32,24]{2,1,0:T(8,128)(2,1)} %bitcast.33) | data formatting | bytes 22020096
  267.2 67.0 %reduce-scatter.4.cloned.1.call-done = bf16[896,768]{1,0:T(8,128)(2,1)} async-done(((bf16[7168,768]{1,0:T(8,128)(2,1)}), bf16[896,768]{1,0:T(8,128)(2,1)}) %reduce-scatter.4.cloned.1.call-update) | async-done | bytes 1376272
  334.3 13.4 %reshape.50 = bf16[896,32,24]{2,1,0:T(8,128)(2,1)} reshape(bf16[896,768]{1,0:T(8,128)(2,1)} %reduce-scatter.4.cloned.1.call-done) | data formatting | bytes 2752512
  347.7 9.7 %copy.52 = bf16[32,24,896]{2,1,0:T(8,128)(2,1)} copy(bf16[32,24,896]{1,0,2:T(8,128)(2,1)} %bitcast.35) | data formatting | bytes 2752512
  357.4 9.7 %all-to-all-start.1 = ((bf16[32,24,896]{2,1,0:T(8,128)(2,1)}), bf16[32,24,896]{2,1,0:T(8,128)(2,1)S(1)}, u32[]{:S(2)}, u32[]{:S(2)}) async-start(bf16[32,24,896]{2,1,0:T(8,128)(2,1)} %copy.52), calls=%async_computation.1 | async-start | bytes 2752512 | tf_op jit(solution)/shard_map/all_to_all | solution.py:51
  367.2 0.1 copy.45
  367.4 3.8 gather_fusion.1
  371.6 0.1 copy.47
  371.8 0.1 copy.50
  371.9 27.9 %all-to-all-done.1 = bf16[32,24,896]{2,1,0:T(8,128)(2,1)S(1)} async-done(((bf16[32,24,896]{2,1,0:T(8,128)(2,1)}), bf16[32,24,896]{2,1,0:T(8,128)(2,1)S(1)}, u32[]{:S(2)}, u32[]{:S(2)}) %all-to-all-start.1) | async-done | bytes 1376288 | tf_op jit(solution)/shard_map/all_to_all | solution.py:51
  399.8 2.0 gather_fusion
  401.9 0.2 reshape.25
  402.1 2.1 multiply_reduce_fusion
  (28 shorter events, 0.8 us)
Async XLA Ops:
  6.5 1.1 copy-start
  6.5 109.8 %all-gather.2.cloned.1.call-start = ((), (), s32[]{:S(2)}) async-start(), calls=%async_computation.3 | async-start | bytes 12386304 | tf_op jit(solution)/shard_map/all_gather | solution.py:43
  53.3 281.0 %reduce-scatter.4.cloned.1.call-start = ((), (), s32[]{:S(2)}) async-start(), calls=%async_computation.4 | async-start | bytes 12386304
  116.3 8.4 %copy-start.5 = (bf16[32,24,7168]{2,1,0:T(8,128)(2,1)S(1)}, bf16[32,24,7168]{2,1,0:T(8,128)(2,1)}, u32[]{:S(2)}) copy-start(bf16[32,24,7168]{2,1,0:T(8,128)(2,1)} %all-gather.2.cloned.1.call-done) | copy-start | bytes 33030148
  116.3 9.4 %copy-start.6 = (bf16[1,7168,256]{2,1,0:T(8,128)(2,1)S(1)}, bf16[1,7168,256]{2,1,0:T(8,128)(2,1)}, u32[]{:S(2)}) copy-start(bf16[1,7168,256]{2,1,0:T(8,128)(2,1)} %param.10) | copy-start | bytes 11010052
  125.7 3.2 copy-start.2
  347.7 19.5 %copy-start.3 = (s32[128,4]{0,1:T(4,128)S(1)}, s32[128,4]{0,1:T(4,128)}, u32[]{:S(2)}) copy-start(s32[128,4]{0,1:T(4,128)} %param.7) | copy-start | bytes 6148
  357.4 42.4 %all-to-all-start.1 = ((bf16[32,24,896]{2,1,0:T(8,128)(2,1)}), bf16[32,24,896]{2,1,0:T(8,128)(2,1)S(1)}, u32[]{:S(2)}, u32[]{:S(2)}) async-start(bf16[32,24,896]{2,1,0:T(8,128)(2,1)} %copy.52), calls=%async_computation.1 | async-start | bytes 2752512 | tf_op jit(solution)/shard_map/all_to_all | solution.py:51
  367.4 4.4 %copy-start.4 = (f32[128,4]{0,1:T(4,128)S(1)}, f32[128,4]{0,1:T(4,128)}, u32[]{:S(2)}) copy-start(f32[128,4]{0,1:T(4,128)} %param.8) | copy-start | bytes 6148
  399.8 4.4 %copy-start.1 = (bf16[128,896]{1,0:T(8,128)(2,1)S(1)}, bf16[128,896]{1,0:T(8,128)(2,1)}, u32[]{:S(2)}) copy-start(bf16[128,896]{1,0:T(8,128)(2,1)} %param.6) | copy-start | bytes 688132
Sparse Core Ops, SparseCore 0:
  53.4 62.8 all-gather.1
  267.4 66.8 reduce-scatter.3
